TPU v7x, 32 devices: a whole 2x2x4 slice. The times are simulated.
32 devices in a mesh: tm: 8 (over y, x, core), lat: 4 (over z).
Axes of the slice: x: 2, y: 2, z: 4, core: 2. Of those that a mesh axis runs over, the one named last changes fastest.
Arguments:
- incr_static: float32 [8, 32, 192, 128], P('tm', 'lat'), may hold values from -6 to 6
- ens_pert: bfloat16 [8, 8, 32, 192, 128], P(None, 'tm', 'lat'), may hold values from -0.59765625 to 0.59765625
- ens_weight: float32 [8, 4, 1024], P(None, 'lat', 'tm'), may hold values from -6 to 6
- column_map: int32 [32, 192], P('lat'), may hold values from 0 to 1023
- sub_steps: int32 [8], P('tm'), may hold values from 1 to 4, 24 in all
- diffusion: bfloat16 [8, 32, 192, 128], P('tm', 'lat'), may hold values from 0.0099487305 to 0.23925781
- mode_in: bfloat16 [4, 128, 128], replicated, may hold values from -0.5 to 0.5
- mode_out: bfloat16 [4, 128, 128], replicated, may hold values from -0.25 to 0.25
- model_precision: bfloat16 [8, 32, 192, 128], P('tm', 'lat'), may hold values from 0.099609375 to 1
- obs_precision: bfloat16 [8, 32, 192, 128], P('tm', 'lat'), may hold values from 0.099609375 to 1
- innovation: bfloat16 [8, 32, 192, 128], P('tm', 'lat'), may hold values from -6 to 6
Outputs:
- grad_static: float32 [8, 32, 192, 128], P('tm', 'lat')
- grad_weight: float32 [8, 4, 1024], P(None, 'lat', 'tm')
Inputs may be any that keep to these rules, and one draw needn't show every extreme that they name: `column_map`: each cell names one of the 1024 weight columns of its own latitude slab. `sub_steps`: the subwindows' step counts add up to 24.
All inputs are finite; a program needn't handle non-finite values. No bound on the sum of `sub_steps` on one device may be relied on, other than what follows from the above.
Results may differ from a plain program's by a relative error of at most 0.0065.
Values may be sent and summed in bfloat16 or wider, within the bound.
A program may use at most 64 MiB of HBM per device.

v0:
```python
import jax
import jax.numpy as jnp
from jax import lax
from jax.sharding import PartitionSpec as P

STEPS = 4


def with_halo(cells, sides, width):
    for axis, dim in sides:
        count = lax.axis_size(axis)
        ends = count - 1
        head = lax.slice_in_dim(cells, 0, width, axis=dim)
        tail = lax.slice_in_dim(cells, cells.shape[dim] - width, cells.shape[dim], axis=dim)
        cells = jnp.concatenate(
            [
                lax.ppermute(tail, axis, [(i, (i + 1) % count) for i in range(ends)]),
                cells,
                lax.ppermute(head, axis, [((i + 1) % count, i) for i in range(ends)]),
            ],
            axis=dim,
        )
    return cells


def from_behind(block, axis, distance):
    devices = range(lax.axis_size(axis))
    route = [(i - distance, i) for i in devices if i - distance in devices]
    return lax.ppermute(block, axis, route)


def laplace_zero(state_field):
    padded = jnp.pad(state_field, ((1, 1), (0, 0), (0, 0)))
    return (
        padded[2:]
        + padded[:-2]
        + jnp.roll(state_field, 1, axis=1)
        + jnp.roll(state_field, -1, axis=1)
        - 4.0 * state_field
    )


def vertical(smoothed, to_modes, from_modes):
    layout = smoothed.shape
    flat = smoothed.astype(jnp.bfloat16).reshape(-1, layout[-1])
    mode_values = jnp.dot(flat, to_modes, preferred_element_type=jnp.float32).astype(jnp.bfloat16)
    return jnp.dot(mode_values, from_modes, preferred_element_type=jnp.float32).reshape(layout)


def forward_deep(state_field, diffuse_wide, step_count, mode_in, mode_out):
    extended = with_halo(state_field, (("lat", 0),), STEPS)
    for section in range(STEPS):
        smoothed = extended + diffuse_wide * laplace_zero(extended)
        advanced = smoothed + vertical(smoothed, mode_in[section], mode_out[section])
        extended = jnp.where(section < step_count, advanced, extended)
    return extended[STEPS:-STEPS]


def adjoint_deep(state_field, diffuse_wide, step_count, mode_in, mode_out):
    extended = with_halo(state_field.astype(jnp.bfloat16), (("lat", 0),), STEPS).astype(
        state_field.dtype
    )
    for section in reversed(range(STEPS)):
        coupled = extended + vertical(extended, mode_out[section].T, mode_in[section].T)
        advanced = coupled + laplace_zero(diffuse_wide * coupled)
        extended = jnp.where(section < step_count, advanced, extended)
    return extended[STEPS:-STEPS]


def body(
    incr_static,
    ens_pert,
    ens_weight,
    column_map,
    sub_steps,
    diffusion,
    mode_in,
    mode_out,
    model_precision,
    obs_precision,
    innovation,
):
    step_count = sub_steps[0]
    gathered = lax.all_gather(ens_weight, "tm", axis=2, tiled=True)
    member_weight = jnp.take(gathered[:, 0, :], column_map, axis=1)
    start_state = incr_static[0] + jnp.sum(
        ens_pert[:, 0].astype(jnp.float32) * member_weight[..., None], axis=0
    )
    precision = model_precision[0].astype(jnp.float32)
    diffuse_wide = with_halo(diffusion[0], (("lat", 0),), STEPS).astype(jnp.float32)
    end_state = forward_deep(start_state, diffuse_wide, step_count, mode_in, mode_out)
    earlier = from_behind(end_state.astype(jnp.bfloat16), "tm", 1).astype(end_state.dtype)
    jump_term = precision * (start_state - earlier)
    following = from_behind(jump_term.astype(jnp.bfloat16), "tm", -1).astype(jump_term.dtype)
    misfit = obs_precision[0].astype(jnp.float32) * (end_state - innovation[0].astype(jnp.float32))
    adjoint_seed = misfit - following
    carried = adjoint_deep(adjoint_seed, diffuse_wide, step_count, mode_in, mode_out)
    gradient = jump_term + carried
    contrib = jnp.sum(ens_pert[:, 0].astype(jnp.float32) * gradient[None], axis=-1)
    columns = gathered.shape[2]
    summed = jax.ops.segment_sum(
        contrib.reshape(contrib.shape[0], -1).T, column_map.reshape(-1), num_segments=columns
    )
    owned_sum = lax.psum_scatter(summed.T[:, None, :], "tm", scatter_dimension=2, tiled=True)
    return (gradient[None], ens_weight + owned_sum)


def solution(mesh):
    return jax.shard_map(
        body,
        mesh=mesh,
        in_specs=(
            P("tm", "lat", None, None),
            P(None, "tm", "lat", None, None),
            P(None, "lat", "tm"),
            P("lat", None),
            P("tm"),
            P("tm", "lat", None, None),
            P(),
            P(),
            P("tm", "lat", None, None),
            P("tm", "lat", None, None),
            P("tm", "lat", None, None),
        ),
        out_specs=(P("tm", "lat", None, None), P(None, "lat", "tm")),
        check_vma=False,
    )
```

profile of v0, /device:TPU:0, one launch (start us, length us, event | category | flops | bytes accessed | tf_op | source)
XLA Modules:
  0.0 153.7 jit_solution(16810483407218309894)
XLA Ops:
  9.4 12.6 %all_gather.3 = f32[8,1,1024]{0,2,1:T(8,128)} all-gather(f32[8,1,128]{0,2,1:T(8,128)S(1)} %copy.17), channel_id=1, replica_groups=mesh['tm'=8,'lat'=4] {'tm'}, dimensions={2}, use_global_device_ids=true | all-gather | bytes 36864 | tf_op jit(solution)/shard_map/all_gather | solution.py:84
  22.1 4.7 %gather_fusion = f32[1536,8]{1,0:T(8,128)} fusion(f32[8,1024]{0,1:T(8,128)} %bitcast.152, s32[2048]{0:T(1024)S(1)} %pad_clamp_fusion), kind=kCustom, calls=%fused_computation | custom fusion | bytes 104448 | tf_op jit(solution)/shard_map/jit(_take)/gather | solution.py:85
  26.9 2.3 %select_bitcast_fusion = f32[8,8,192]{0,2,1:T(8,128)} fusion(f32[8,192,8]{2,1,0:T(8,128)} %bitcast.154, pred[8,192]{1,0:T(8,128)(4,1)S(1)} %compare_and_fusion), kind=kLoop, calls=%fused_computation.104 | loop fusion | flops 12288 | bytes 99840 | tf_op jit(solution)/shard_map/jit(_take)/select_n | solution.py:85
  29.1 1.4 copy.18
  30.6 2.0 %fusion = f32[8,192,128]{2,1,0:T(8,128)S(1)} fusion(bf16[8,1,8,192,128]{4,3,2,1,0:T(8,128)(2,1)S(1)} %copy-done.1, f32[8,8,192]{2,1,0:T(8,128)S(1)} %copy.18), kind=kLoop, calls=%fused_computation.4 | loop fusion | flops 4521984 | bytes 3981312 | tf_op jit(solution)/shard_map/reduce_sum | solution.py:86
  32.8 1.3 collective-permute-start.1
  34.1 4.6 %collective-permute-start = (f32[4,192,128]{2,1,0:T(8,128)S(1)}, f32[4,192,128]{2,1,0:T(8,128)S(1)}, u32[]{:S(2)}, u32[]{:S(2)}) collective-permute-start(f32[4,192,128]{2,1,0:T(8,128)S(1)} %get-tuple-element.56), channel_id=1, source_target_pairs={{0,1},{1,2},{2,3},{4,5},{5,6},{6,7},{8,9},{9,10},{10,11},{12,13},{... | collective-permute-start | bytes 1179656 | tf_op jit(solution)/shard_map/ppermute | solution.py:17
  38.7 1.3 collective-permute-start.3
  40.0 4.6 %collective-permute-start.2 = (bf16[4,192,128]{2,1,0:T(8,128)(2,1)S(1)}, bf16[4,192,128]{2,1,0:T(8,128)(2,1)S(1)}, u32[]{:S(2)}, u32[]{:S(2)}) collective-permute-start(bf16[4,192,128]{2,1,0:T(8,128)(2,1)S(1)} %get-tuple-element.60), channel_id=1, source_target_pairs={{0,1},{1,2},{2,3},{4,5},{5,6},{6,7},{8,9},{9,10},{10,11},{12,13},{... | collective-permute-start | bytes 589832 | tf_op jit(solution)/shard_map/ppermute | solution.py:17
  45.2 1.4 collective-permute-done.1
  46.7 1.5 collective-permute-done
  48.6 1.6 %collective-permute-done.3 = bf16[4,192,128]{2,1,0:T(8,128)(2,1)S(1)} collective-permute-done((bf16[4,192,128]{2,1,0:T(8,128)(2,1)S(1)}, bf16[4,192,128]{2,1,0:T(8,128)(2,1)S(1)}, u32[]{:S(2)}, u32[]{:S(2)}) %collective-permute-start.3) | collective-permute-done | bytes 196640 | tf_op jit(solution)/shard_map/ppermute | solution.py:19
  59.0 1.4 collective-permute-start.4
  60.4 1.3 collective-permute-done.4
  61.9 1.3 collective-permute-start.5
  63.2 7.3 %collective-permute-done.5 = bf16[8,192,128]{2,1,0:T(8,128)(2,1)S(1)} collective-permute-done((bf16[8,192,128]{2,1,0:T(8,128)(2,1)S(1)}, bf16[8,192,128]{2,1,0:T(8,128)(2,1)S(1)}, u32[]{:S(2)}, u32[]{:S(2)}) %collective-permute-start.5) | collective-permute-done | bytes 393248 | tf_op jit(solution)/shard_map/ppermute | solution.py:29
  71.5 1.3 collective-permute-start.7
  72.8 5.2 %collective-permute-start.6 = (bf16[4,192,128]{2,1,0:T(8,128)(2,1)}, bf16[4,192,128]{2,1,0:T(8,128)(2,1)S(1)}, u32[]{:S(2)}, u32[]{:S(2)}) collective-permute-start(bf16[4,192,128]{2,1,0:T(8,128)(2,1)} %get-tuple-element.58), channel_id=1, source_target_pairs={{0,1},{1,2},{2,3},{4,5},{5,6},{6,7},{8,9},{9,10},{10,11},{12,13},{... | collective-permute-start | bytes 589832 | tf_op jit(solution)/shard_map/ppermute | solution.py:17
  78.1 1.6 %collective-permute-done.7 = bf16[4,192,128]{2,1,0:T(8,128)(2,1)S(1)} collective-permute-done((bf16[4,192,128]{2,1,0:T(8,128)(2,1)}, bf16[4,192,128]{2,1,0:T(8,128)(2,1)S(1)}, u32[]{:S(2)}, u32[]{:S(2)}) %collective-permute-start.7) | collective-permute-done | bytes 196640 | tf_op jit(solution)/shard_map/ppermute | solution.py:19
  79.7 1.6 %collective-permute-done.6 = bf16[4,192,128]{2,1,0:T(8,128)(2,1)S(1)} collective-permute-done((bf16[4,192,128]{2,1,0:T(8,128)(2,1)}, bf16[4,192,128]{2,1,0:T(8,128)(2,1)S(1)}, u32[]{:S(2)}, u32[]{:S(2)}) %collective-permute-start.6) | collective-permute-done | bytes 196640 | tf_op jit(solution)/shard_map/ppermute | solution.py:17
  89.5 1.2 copy-done.2
  90.7 2.3 %fusion.1 = f32[8,8,192]{2,1,0:T(8,128)S(1)} fusion(bf16[8,1,8,192,128]{4,3,2,1,0:T(8,128)(2,1)S(1)} %copy-done.2, f32[8,192,128]{2,1,0:T(8,128)S(1)} %fusion.39), kind=kLoop, calls=%fused_computation.5 | loop fusion | flops 4706304 | bytes 3981312 | tf_op jit(solution)/shard_map/reduce_sum | solution.py:99
  93.3 9.5 %scatter_custom_fusion = f32[1024,8]{1,0:T(8,128)} fusion(s32[1536]{0:T(1024)S(1)} %reshape.97, f32[1536,8]{1,0:T(8,128)S(1)} %bitcast.155, f32[]{:T(128)} %constant.28.clone.1), kind=kCustom, calls=%fused_computation.106 | custom fusion | flops 12288 | bytes 32772 | tf_op jit(solution)/shard_map/scatter-add | solution.py:101
  102.8 42.5 %reduce-scatter.2.cloned.1.call-done = f32[8,1,128]{0,2,1:T(8,128)} async-done(((f32[8,1,1024]{0,2,1:T(8,128)}), f32[8,1,128]{0,2,1:T(8,128)}) %reduce-scatter.2.cloned.1.call-update) | async-done | bytes 4112 | tf_op jit(solution)/shard_map/reduce_scatter | solution.py:104
  (83 shorter events, 22.6 us)
Async XLA Ops:
  7.2 138.2 %reduce-scatter.2.cloned.1.call-start = ((), (), s32[]{:S(2)}) async-start(), calls=%async_computation.1 | async-start | bytes 589824 | tf_op jit(solution)/shard_map/reduce_scatter | solution.py:104
  9.4 21.2 %copy-start.1 = (bf16[8,1,8,192,128]{4,3,2,1,0:T(8,128)(2,1)S(1)}, bf16[8,1,8,192,128]{4,3,2,1,0:T(8,128)(2,1)}, u32[]{:S(2)}) copy-start(bf16[8,1,8,192,128]{4,3,2,1,0:T(8,128)(2,1)} %param.12) | copy-start | bytes 9437188
  30.6 2.0 %copy-start.5 = (f32[1,8,192,128]{3,2,1,0:T(8,128)S(1)}, f32[1,8,192,128]{3,2,1,0:T(8,128)}, u32[]{:S(2)}) copy-start(f32[1,8,192,128]{3,2,1,0:T(8,128)} %param.11) | copy-start | bytes 2359300
  32.6 6.0 %copy-start = (bf16[1,8,192,128]{3,2,1,0:T(8,128)(2,1)S(1)}, bf16[1,8,192,128]{3,2,1,0:T(8,128)(2,1)}, u32[]{:S(2)}) copy-start(bf16[1,8,192,128]{3,2,1,0:T(8,128)(2,1)} %param.16) | copy-start | bytes 1179652
  32.8 13.9 %collective-permute-start.1 = (f32[4,192,128]{2,1,0:T(8,128)S(1)}, f32[4,192,128]{2,1,0:T(8,128)S(1)}, u32[]{:S(2)}, u32[]{:S(2)}) collective-permute-start(f32[4,192,128]{2,1,0:T(8,128)S(1)} %get-tuple-element.57), channel_id=1, source_target_pairs={{1,0},{2,1},{3,2},{5,4},{6,5},{7,6},{9,8},{10,9},{11,10},{13,12},{... | collective-permute-start | bytes 1179656 | tf_op jit(solution)/shard_map/ppermute | solution.py:19
  34.1 14.0 %collective-permute-start = (f32[4,192,128]{2,1,0:T(8,128)S(1)}, f32[4,192,128]{2,1,0:T(8,128)S(1)}, u32[]{:S(2)}, u32[]{:S(2)}) collective-permute-start(f32[4,192,128]{2,1,0:T(8,128)S(1)} %get-tuple-element.56), channel_id=1, source_target_pairs={{0,1},{1,2},{2,3},{4,5},{5,6},{6,7},{8,9},{9,10},{10,11},{12,13},{... | collective-permute-start | bytes 1179656 | tf_op jit(solution)/shard_map/ppermute | solution.py:17
  38.7 11.6 %collective-permute-start.3 = (bf16[4,192,128]{2,1,0:T(8,128)(2,1)S(1)}, bf16[4,192,128]{2,1,0:T(8,128)(2,1)S(1)}, u32[]{:S(2)}, u32[]{:S(2)}) collective-permute-start(bf16[4,192,128]{2,1,0:T(8,128)(2,1)S(1)} %get-tuple-element.61), channel_id=1, source_target_pairs={{1,0},{2,1},{3,2},{5,4},{6,5},{7,6},{9,8},{10,9},{11,10},{13,12},{... | collective-permute-start | bytes 589832 | tf_op jit(solution)/shard_map/ppermute | solution.py:19
  40.0 11.4 %collective-permute-start.2 = (bf16[4,192,128]{2,1,0:T(8,128)(2,1)S(1)}, bf16[4,192,128]{2,1,0:T(8,128)(2,1)S(1)}, u32[]{:S(2)}, u32[]{:S(2)}) collective-permute-start(bf16[4,192,128]{2,1,0:T(8,128)(2,1)S(1)} %get-tuple-element.60), channel_id=1, source_target_pairs={{0,1},{1,2},{2,3},{4,5},{5,6},{6,7},{8,9},{9,10},{10,11},{12,13},{... | collective-permute-start | bytes 589832 | tf_op jit(solution)/shard_map/ppermute | solution.py:17
  51.5 0.9 copy-start.7
  52.1 0.9 copy-start.6
  58.8 3.0 %copy-start.4 = (bf16[1,8,192,128]{3,2,1,0:T(8,128)(2,1)S(1)}, bf16[1,8,192,128]{3,2,1,0:T(8,128)(2,1)}, u32[]{:S(2)}) copy-start(bf16[1,8,192,128]{3,2,1,0:T(8,128)(2,1)} %param.19) | copy-start | bytes 1179652
  58.9 11.5 %copy-start.8 = (bf16[1,8,192,128]{3,2,1,0:T(8,128)(2,1)S(1)}, bf16[1,8,192,128]{3,2,1,0:T(8,128)(2,1)}, u32[]{:S(2)}) copy-start(bf16[1,8,192,128]{3,2,1,0:T(8,128)(2,1)} %param.21) | copy-start | bytes 1179652
  59.0 11.5 %copy-start.9 = (bf16[1,8,192,128]{3,2,1,0:T(8,128)(2,1)S(1)}, bf16[1,8,192,128]{3,2,1,0:T(8,128)(2,1)}, u32[]{:S(2)}) copy-start(bf16[1,8,192,128]{3,2,1,0:T(8,128)(2,1)} %param.20) | copy-start | bytes 1179652
  59.0 2.8 %collective-permute-start.4 = (bf16[8,192,128]{2,1,0:T(8,128)(2,1)S(1)}, bf16[8,192,128]{2,1,0:T(8,128)(2,1)S(1)}, u32[]{:S(2)}, u32[]{:S(2)}) collective-permute-start(bf16[8,192,128]{2,1,0:T(8,128)(2,1)S(1)} %get-tuple-element.12), channel_id=1, source_target_pairs={{0,4},{4,8},{8,12},{12,16},{16,20},{20,24},{24,28},{1,5},{5,9},{9,... | collective-permute-start | bytes 1179656 | tf_op jit(solution)/shard_map/ppermute | solution.py:29
  61.9 8.6 %collective-permute-start.5 = (bf16[8,192,128]{2,1,0:T(8,128)(2,1)S(1)}, bf16[8,192,128]{2,1,0:T(8,128)(2,1)S(1)}, u32[]{:S(2)}, u32[]{:S(2)}) collective-permute-start(bf16[8,192,128]{2,1,0:T(8,128)(2,1)S(1)} %fusion.46), channel_id=1, source_target_pairs={{4,0},{8,4},{12,8},{16,12},{20,16},{24,20},{28,24},{5,1},{9,5},{13... | collective-permute-start | bytes 1179656 | tf_op jit(solution)/shard_map/ppermute | solution.py:29
  70.5 7.5 %copy-start.10 = (s32[8,192]{1,0:T(8,128)S(1)}, s32[8,192]{1,0:T(8,128)}, u32[]{:S(2)}) copy-start(s32[8,192]{1,0:T(8,128)} %param.14) | copy-start | bytes 18436
  71.5 8.2 %collective-permute-start.7 = (bf16[4,192,128]{2,1,0:T(8,128)(2,1)}, bf16[4,192,128]{2,1,0:T(8,128)(2,1)S(1)}, u32[]{:S(2)}, u32[]{:S(2)}) collective-permute-start(bf16[4,192,128]{2,1,0:T(8,128)(2,1)} %get-tuple-element.59), channel_id=1, source_target_pairs={{1,0},{2,1},{3,2},{5,4},{6,5},{7,6},{9,8},{10,9},{11,10},{13,12},{... | collective-permute-start | bytes 589832 | tf_op jit(solution)/shard_map/ppermute | solution.py:19
  72.8 8.5 %collective-permute-start.6 = (bf16[4,192,128]{2,1,0:T(8,128)(2,1)}, bf16[4,192,128]{2,1,0:T(8,128)(2,1)S(1)}, u32[]{:S(2)}, u32[]{:S(2)}) collective-permute-start(bf16[4,192,128]{2,1,0:T(8,128)(2,1)} %get-tuple-element.58), channel_id=1, source_target_pairs={{0,1},{1,2},{2,3},{4,5},{5,6},{6,7},{8,9},{9,10},{10,11},{12,13},{... | collective-permute-start | bytes 589832 | tf_op jit(solution)/shard_map/ppermute | solution.py:17
  88.8 1.9 %copy-start.2 = (bf16[8,1,8,192,128]{4,3,2,1,0:T(8,128)(2,1)S(1)}, bf16[8,1,8,192,128]{4,3,2,1,0:T(8,128)(2,1)}, u32[]{:S(2)}) copy-start(bf16[8,1,8,192,128]{4,3,2,1,0:T(8,128)(2,1)} %param.12) | copy-start | bytes 9437188
  90.7 2.3 %copy-start.3 = (f32[8,192,128]{2,1,0:T(8,128)}, f32[8,192,128]{2,1,0:T(8,128)S(1)}, u32[]{:S(2)}) copy-start(f32[8,192,128]{2,1,0:T(8,128)S(1)} %fusion.39) | copy-start | bytes 2359300
Sparse Core Ops, SparseCore 0:
  103.0 42.3 reduce-scatter.1
where the time goes:
time: 154 us
  waiting for transfers between devices  60.1 us (39%)
  other arithmetic  25 us (16%)
  starting transfers between devices  21 us (14%)
  between operations  15.2 us (10%)
  local copies, waits for them, and re-layouts  13.9 us (9%)
  blocking collectives  12.6 us (8%)
  matrix products  5.84 us (4%)
    reduce_scatter x1, waiting for transfers between devices, body(): lax.psum_scatter(summed.T[:, None, :], 'tm', scatter_dimension=2, tiled=T...  42.5 us
    ppermute x3, starting transfers between devices, with_halo(): lax.ppermute(tail, axis, [(i, (i + 1) % count) for i in range(ends)])  14.3 us
    all_gather x1, blocking collectives, body(): gathered = lax.all_gather(ens_weight, 'tm', axis=2, tiled=True)  12.6 us
    scatter-add x1, other arithmetic, body(): jax.ops.segment_sum(contrib.reshape(contrib.shape[0], -1).T, column_map.r...  9.51 us
    ppermute x2, waiting for transfers between devices, from_behind(): return lax.ppermute(block, axis, route)  8.63 us
    convert_element_type x7, other arithmetic, vertical(): flat = smoothed.astype(jnp.bfloat16).reshape(-1, layout[-1])  5.22 us
    ppermute x3, waiting for transfers between devices, with_halo(): lax.ppermute(head, axis, [((i + 1) % count, i) for i in range(ends)])  4.73 us
    gather x1, local copies, waits for them, and re-layouts, body(): member_weight = jnp.take(gathered[:, 0, :], column_map, axis=1)  4.73 us
  transfers between devices with their start and end apart: 9, of which 9 were waited for; matrix products, arithmetic and copies ran while one was open for 0% of the time, Pallas kernels for 0%

commit v1 on v0

v1 whole, which is shorter than its diff:
```python
import jax
import jax.numpy as jnp
from jax import lax
from jax.experimental import pallas as pl
from jax.experimental.pallas import tpu as pltpu
from jax.sharding import PartitionSpec as P

MESH = pl.DeviceIdType.MESH
F32, BF16 = jnp.float32, jnp.bfloat16
LAST = (((1,), (1,)), ((), ()))


def halves(x):
    high = x.astype(BF16)
    low = (x - high.astype(F32)).astype(BF16)
    return jnp.concatenate([high, low], axis=0)


def kernel(
    tm_count, lat_count, sizes,
    steps_ref, incr_h, pert_h, weight_h, cmap_h, diff_h, min_h, mout_h, prec_h, obs_h, innov_h,
    grad_h, gw_ref,
    incr, pert, gathered, cmap, cpad, diff, m_in, m_out, prec, obs, innov,
    onehot, start, start_bf, a_buf, b_buf, state_halo, start_next, prec_next,
    end_bf, end_prev, u_buf, seed_bf, seed_halo, c_buf, w_buf, mw_t, contrib, grad,
    term_send, term_recv, local_sem, send_sem, recv_sem, ag_send, ag_recv, rs_send, rs_recv,
):
    H, R, LON, LEV, MEM, CW = sizes
    C = CW * tm_count
    PAD = cpad.shape[1]
    me_t, me_l = lax.axis_index("tm"), lax.axis_index("lat")
    has_up, has_down = me_l > 0, me_l < lat_count - 1
    has_prev, has_next = me_t > 0, me_t < tm_count - 1

    def local(i, src, dst):
        return pltpu.make_async_copy(src, dst, local_sem.at[i])

    def remote(i, src, dst, tm, lat):
        return pltpu.make_async_remote_copy(
            src_ref=src, dst_ref=dst, send_sem=send_sem.at[i], recv_sem=recv_sem.at[i],
            device_id=(tm, lat), device_id_type=MESH,
        )

    loads = dict(
        weight=local(0, weight_h, gathered.at[me_t]),
        cmap=local(1, cmap_h, cmap),
        pert=local(2, pert_h.at[:, 0], pert),
        incr=local(3, incr_h.at[0], incr),
        diff=local(4, diff_h.at[0], diff.at[pl.ds(H, R)]),
        m_in=local(5, min_h, m_in),
        m_out=local(6, mout_h, m_out),
        prec=local(7, prec_h.at[0], prec),
        obs=local(8, obs_h.at[0], obs),
        innov=local(9, innov_h.at[0], innov),
    )
    for copy in loads.values():
        copy.start()

    barrier = pltpu.get_barrier_semaphore()
    for d in range(1, tm_count):
        pl.semaphore_signal(barrier, inc=1, device_id=(lax.rem(me_t + d, tm_count), me_l), device_id_type=MESH)

    @pl.when(has_up)
    def _():
        pl.semaphore_signal(barrier, inc=1, device_id=(me_t, me_l - 1), device_id_type=MESH)

    @pl.when(has_down)
    def _():
        pl.semaphore_signal(barrier, inc=1, device_id=(me_t, me_l + 1), device_id_type=MESH)

    @pl.when(jnp.logical_not(has_up))
    def _():
        diff[0:H] = jnp.zeros((H, LON, LEV), BF16)
        state_halo[0] = jnp.zeros((H, LON, LEV), BF16)
        seed_halo[0] = jnp.zeros((H, LON, LEV), BF16)

    @pl.when(jnp.logical_not(has_down))
    def _():
        diff[H + R:2 * H + R] = jnp.zeros((H, LON, LEV), BF16)
        state_halo[1] = jnp.zeros((H, LON, LEV), BF16)
        seed_halo[1] = jnp.zeros((H, LON, LEV), BF16)

    @pl.when(jnp.logical_not(has_prev))
    def _():
        end_prev[...] = jnp.zeros((R, LON, LEV), BF16)

    @pl.when(jnp.logical_not(has_next))
    def _():
        start_next[...] = jnp.zeros((R, LON, LEV), BF16)
        prec_next[...] = jnp.zeros((R, LON, LEV), BF16)

    loads["weight"].wait()
    pl.semaphore_wait(barrier, tm_count - 1 + has_up.astype(jnp.int32) + has_down.astype(jnp.int32))

    def spread(d):
        peer = lax.rem(me_t + d, tm_count)
        return pltpu.make_async_remote_copy(
            src_ref=gathered.at[me_t], dst_ref=gathered.at[me_t], send_sem=ag_send.at[d],
            recv_sem=ag_recv.at[d], device_id=(peer, me_l), device_id_type=MESH,
        )

    def term(d):
        peer = lax.rem(me_t + d, tm_count)
        return pltpu.make_async_remote_copy(
            src_ref=term_send.at[peer], dst_ref=term_recv.at[me_t], send_sem=rs_send.at[d],
            recv_sem=rs_recv.at[d], device_id=(peer, me_l), device_id_type=MESH,
        )

    for d in range(1, tm_count):
        spread(d).start()

    diff_up = remote(0, diff_h.at[0, pl.ds(0, H)], diff.at[pl.ds(H + R, H)], me_t, me_l - 1)
    diff_down = remote(1, diff_h.at[0, pl.ds(R - H, H)], diff.at[pl.ds(0, H)], me_t, me_l + 1)
    prec_back = remote(2, prec_h.at[0], prec_next, me_t - 1, me_l)
    start_back = remote(3, start_bf, start_next, me_t - 1, me_l)
    state_up = remote(4, start_bf.at[pl.ds(0, H)], state_halo.at[1], me_t, me_l - 1)
    state_down = remote(5, start_bf.at[pl.ds(R - H, H)], state_halo.at[0], me_t, me_l + 1)
    end_on = remote(6, end_bf, end_prev, me_t + 1, me_l)
    seed_up = remote(7, seed_bf.at[pl.ds(0, H)], seed_halo.at[1], me_t, me_l - 1)
    seed_down = remote(8, seed_bf.at[pl.ds(R - H, H)], seed_halo.at[0], me_t, me_l + 1)

    def go(copy, there):
        @pl.when(there)
        def _():
            copy.start()

    def sent(copy, there):
        @pl.when(there)
        def _():
            copy.wait_send()

    def got(copy, there):
        @pl.when(there)
        def _():
            copy.wait_recv()

    go(diff_up, has_up)
    go(diff_down, has_down)
    go(prec_back, has_prev)

    loads["cmap"].wait()
    cpad[...] = jnp.full(cpad.shape, -1, jnp.int32)
    cpad[:, 0:LON] = cmap[...]
    contrib[...] = jnp.zeros(contrib.shape, F32)
    LANES = PAD
    CH = 128 if C % 128 == 0 else C

    def indicate(chunk, carry):
        base = pl.multiple_of(chunk * CH, CH)
        rows = lax.broadcasted_iota(jnp.int32, (CH, LANES), 0) + base
        for i in range(R):
            hit = jnp.where(rows == cpad[i:i + 1, :], 1.0, 0.0).astype(BF16)
            onehot[pl.ds(base, CH), i * LANES:(i + 1) * LANES] = hit
        return carry

    lax.fori_loop(0, C // CH, indicate, 0)

    for d in range(1, tm_count):
        spread(d).wait_recv()
    weights = jnp.concatenate([gathered[p] for p in range(tm_count)], axis=1)
    picked = jnp.dot(halves(weights), onehot[...], preferred_element_type=F32)
    mw_t[...] = jnp.transpose(picked[0:MEM] + picked[MEM:2 * MEM])

    loads["pert"].wait()
    loads["incr"].wait()

    def begin(i, carry):
        cols = mw_t[pl.ds(pl.multiple_of(i * LANES, LANES), LON), :]
        row = incr[i]
        for k in range(MEM):
            row = row + pert[k, i].astype(F32) * cols[:, k:k + 1]
        start[i] = row
        a_buf[i + H] = row
        start_bf[i] = row.astype(BF16)
        return carry

    lax.fori_loop(0, H, begin, 0)
    go(state_up, has_up)
    lax.fori_loop(H, R - H, begin, 0)
    lax.fori_loop(R - H, R, begin, 0)
    go(state_down, has_down)
    go(start_back, has_prev)

    step_count = steps_ref[0]
    loads["diff"].wait()
    loads["m_in"].wait()
    loads["m_out"].wait()

    def forward_row(n, src, dst, r):
        here = src[r]
        lap = src[r - 1] + src[r + 1] + pltpu.roll(here, 1, 0) + pltpu.roll(here, LON - 1, 0) - 4.0 * here
        smoothed = here + diff[r].astype(F32) * lap
        modes = jnp.dot(smoothed.astype(BF16), m_in[n], preferred_element_type=F32).astype(BF16)
        advanced = smoothed + jnp.dot(modes, m_out[n], preferred_element_type=F32)
        result = jnp.where(n < step_count, advanced, here)
        dst[r] = result
        return result

    def buffers(n):
        return (a_buf, b_buf) if n % 2 == 0 else (b_buf, a_buf)

    def forward_inner(n):
        src, dst = buffers(n)
        first, count = H + n + 1, R - 2 * n - 2

        def pair(i, carry):
            forward_row(n, src, dst, first + i)
            forward_row(n, src, dst, first + count // 2 + i)
            return carry

        if count > 0:
            lax.fori_loop(0, count // 2, pair, 0)

    def forward_edges(n):
        src, dst = buffers(n)

        def pair(i, carry):
            forward_row(n, src, dst, n + 1 + i)
            forward_row(n, src, dst, H + R - n - 1 + i)
            return carry

        lax.fori_loop(0, H, pair, 0)

    for n in range(H - 1):
        forward_inner(n)
    got(diff_up, has_down)
    got(diff_down, has_up)
    got(state_up, has_down)
    got(state_down, has_up)

    def widen(i, carry):
        a_buf[i] = state_halo[0, i].astype(F32)
        a_buf[i + H + R] = state_halo[1, i].astype(F32)
        return carry

    lax.fori_loop(0, H, widen, 0)
    for n in range(H - 1):
        forward_edges(n)
    loads["obs"].wait()
    loads["innov"].wait()
    got(prec_back, has_next)
    got(start_back, has_next)
    src, dst = buffers(H - 1)

    def finish_row(i):
        end = forward_row(H - 1, src, dst, i + H)
        misfit = obs[i].astype(F32) * (end - innov[i].astype(F32))
        seed = misfit - prec_next[i].astype(F32) * (start_next[i].astype(F32) - end)
        end_bf[i] = end.astype(BF16)
        u_buf[i + H] = seed
        seed_bf[i] = seed.astype(BF16)

    def finish(i, carry):
        finish_row(2 * i)
        finish_row(2 * i + 1)
        return carry

    lax.fori_loop(0, H // 2, finish, 0)
    go(seed_up, has_up)
    lax.fori_loop(H // 2, R // 2, finish, 0)
    go(seed_down, has_down)
    go(end_on, has_next)

    def couple_row(m, r):
        n = H - 1 - m
        here = u_buf[r]
        modes = lax.dot_general(here.astype(BF16), m_out[n], LAST, preferred_element_type=F32).astype(BF16)
        coupled = here + lax.dot_general(modes, m_in[n], LAST, preferred_element_type=F32)
        c_buf[m % 2, r] = coupled
        w_buf[m % 2, r] = diff[r].astype(F32) * coupled

    def spread_row(m, r):
        w = w_buf.at[m % 2]
        here = w[r]
        lap = w[r - 1] + w[r + 1] + pltpu.roll(here, 1, 0) + pltpu.roll(here, LON - 1, 0) - 4.0 * here
        u_buf[r] = jnp.where(H - 1 - m < step_count, c_buf[m % 2, r] + lap, u_buf[r])

    def two(row, m, first, second, count):
        def pair(i, carry):
            row(m, first + i)
            row(m, second + i)
            return carry

        if count > 0:
            lax.fori_loop(0, count, pair, 0)

    for m in range(H):
        inside = (R - 2 * m) // 2
        two(couple_row, m, H + m, H + m + inside, inside)
        inside = (R - 2 * m - 2) // 2
        two(spread_row, m, H + m + 1, H + m + 1 + inside, inside)
    got(seed_up, has_down)
    got(seed_down, has_up)

    def widen_seed(i, carry):
        u_buf[i] = seed_halo[0, i].astype(F32)
        u_buf[i + H + R] = seed_halo[1, i].astype(F32)
        return carry

    lax.fori_loop(0, H, widen_seed, 0)
    for m in range(H):
        two(couple_row, m, m, H + R - m, H)
        two(spread_row, m, m + 1, H + R - m - 1, H)

    got(end_on, has_prev)
    loads["prec"].wait()
    lane = lax.broadcasted_iota(jnp.int32, (MEM, MEM * LEV), 1)
    member = lax.broadcasted_iota(jnp.int32, (MEM, MEM * LEV), 0) * LEV
    own = jnp.where((lane >= member) & (lane < member + LEV), 1.0, 0.0).astype(BF16)

    for i in range(R):
        jump = prec[i].astype(F32) * (start[i] - end_prev[i].astype(F32))
        total = jump + u_buf[i + H]
        grad[i] = total
        terms = jnp.concatenate([(pert[k, i].astype(F32) * total).astype(BF16) for k in range(MEM)], axis=1)
        contrib[:, i * LANES:i * LANES + LON] = lax.dot_general(own, terms, LAST, preferred_element_type=F32)

    store = local(10, grad, grad_h.at[0])
    store.start()
    sums = lax.dot_general(halves(contrib[...]), onehot[...], LAST, preferred_element_type=F32)
    sums = sums[0:MEM] + sums[MEM:2 * MEM]
    for p in range(tm_count):
        term_send[p] = sums[:, p * CW:(p + 1) * CW]
    for d in range(1, tm_count):
        term(d).start()
    result = gathered[me_t] + term_send[me_t]
    for d in range(1, tm_count):
        term(d).wait_recv()
    for d in range(1, tm_count):
        result = result + term_recv[lax.rem(me_t + d, tm_count)]
    gw_ref[...] = result

    for d in range(1, tm_count):
        spread(d).wait_send()
        term(d).wait_send()
    for copy in (diff_up, state_up, seed_up):
        sent(copy, has_up)
    for copy in (diff_down, state_down, seed_down):
        sent(copy, has_down)
    sent(prec_back, has_prev)
    sent(start_back, has_prev)
    sent(end_on, has_next)
    store.wait()


def solution(mesh):
    tm_count, lat_count = mesh.shape["tm"], mesh.shape["lat"]

    def body(incr, pert, weight, cmap, steps, diffusion, m_in, m_out, prec, obs, innov):
        _, R, LON, LEV = incr.shape
        MEM, _, CW = weight.shape
        H = m_in.shape[0]
        PAD = -(-LON // 128) * 128
        field = lambda rows, kind: pltpu.VMEM((rows, LON, LEV), kind)
        wide = 2 * H + R
        scratch = [
            field(R, F32),
            pltpu.VMEM((MEM, R, LON, LEV), BF16),
            pltpu.VMEM((tm_count, MEM, CW), F32),
            pltpu.VMEM((R, LON), jnp.int32),
            pltpu.VMEM((R, PAD), jnp.int32),
            field(wide, BF16),
            pltpu.VMEM(m_in.shape, BF16),
            pltpu.VMEM(m_out.shape, BF16),
            field(R, BF16), field(R, BF16), field(R, BF16),
            pltpu.VMEM((CW * tm_count, R * PAD), BF16),
            field(R, F32), field(R, BF16), field(wide, F32), field(wide, F32),
            pltpu.VMEM((2, H, LON, LEV), BF16),
            field(R, BF16), field(R, BF16), field(R, BF16), field(R, BF16),
            field(wide, F32), field(R, BF16),
            pltpu.VMEM((2, H, LON, LEV), BF16),
            pltpu.VMEM((2, wide, LON, LEV), F32),
            pltpu.VMEM((2, wide, LON, LEV), F32),
            pltpu.VMEM((R * PAD, MEM), F32),
            pltpu.VMEM((MEM, R * PAD), F32),
            field(R, F32),
            pltpu.VMEM((tm_count, MEM, CW), F32),
            pltpu.VMEM((tm_count, MEM, CW), F32),
            pltpu.SemaphoreType.DMA((11,)),
            pltpu.SemaphoreType.DMA((9,)),
            pltpu.SemaphoreType.DMA((9,)),
        ] + [pltpu.SemaphoreType.DMA((tm_count,))] * 4

        def run(*refs):
            kernel(tm_count, lat_count, (H, R, LON, LEV, MEM, CW), *refs)

        grad, owned = pl.pallas_call(
            run,
            out_shape=(
                jax.ShapeDtypeStruct(incr.shape, F32),
                jax.ShapeDtypeStruct((MEM, CW), F32),
            ),
            in_specs=[pl.BlockSpec(memory_space=pltpu.SMEM)] + [pl.BlockSpec(memory_space=pl.ANY)] * 10,
            out_specs=(pl.BlockSpec(memory_space=pl.ANY), pl.BlockSpec(memory_space=pltpu.VMEM)),
            scratch_shapes=scratch,
            compiler_params=pltpu.CompilerParams(
                collective_id=0, has_side_effects=True, vmem_limit_bytes=60 * 1024 * 1024
            ),
        )(steps, incr, pert, weight[:, 0], cmap, diffusion, m_in, m_out, prec, obs, innov)
        return grad, owned[:, None]

    return jax.shard_map(
        body,
        mesh=mesh,
        in_specs=(
            P("tm", "lat", None, None),
            P(None, "tm", "lat", None, None),
            P(None, "lat", "tm"),
            P("lat", None),
            P("tm"),
            P("tm", "lat", None, None),
            P(),
            P(),
            P("tm", "lat", None, None),
            P("tm", "lat", None, None),
            P("tm", "lat", None, None),
        ),
        out_specs=(P("tm", "lat", None, None), P(None, "lat", "tm")),
        check_vma=False,
    )
```

time: 154 us -> 44.2 us (0.29)
  waiting for transfers between devices: 60.1 us -> 0 us
  Pallas kernels: 0 us -> 39.3 us
  other arithmetic: 25 us -> 0 us
  starting transfers between devices: 21 us -> 0 us
  between operations: 15.2 us -> 1.29 us
  blocking collectives: 12.6 us -> 0 us
  local copies, waits for them, and re-layouts: 13.9 us -> 3.34 us
  matrix products: 5.84 us -> 0 us
    reduce_scatter x1 -> x0, waiting for transfers between devices: 42.5 us -> none  [body(): lax.psum_scatter(summed.T[:, None, :], 'tm', scatter_dimension=2, tiled=T...]
    pallas_call x0 -> x1, Pallas kernels: none -> 39.3 us  [body(): pl.pallas_call(run, out_shape=(jax.ShapeDtypeStruct(incr.shape, F32), jax...]
    ppermute x8 -> x0, starting transfers between devices: 20.9 us -> none  [the longest x3 14.3 us: with_halo(): lax.ppermute(tail, axis, [(i, (i + 1) % count) for i in range(ends)])]
    ppermute x8 -> x0, waiting for transfers between devices: 17.6 us -> none  [the longest x2 8.63 us: from_behind(): return lax.ppermute(block, axis, route)]
    all_gather x1 -> x0, blocking collectives: 12.6 us -> none  [body(): gathered = lax.all_gather(ens_weight, 'tm', axis=2, tiled=True)]
    scatter-add x1 -> x0, other arithmetic: 9.51 us -> none  [body(): jax.ops.segment_sum(contrib.reshape(contrib.shape[0], -1).T, column_map.r...]
    dot_general x16 -> x0, matrix products: 5.84 us -> none  [the longest x8 3.01 us: vertical(): jnp.dot(mode_values, from_modes, preferred_element_type=jnp.float32)]
    convert_element_type x10 -> x0, other arithmetic: 5.73 us -> none  [the longest x7 5.22 us: vertical(): flat = smoothed.astype(jnp.bfloat16).reshape(-1, layout[-1])]
  transfers between devices with their start and end apart: 9 -> 0, of which waited for: 9 -> 0; matrix products, arithmetic and copies ran while one was open for 0% -> 0% of each run, Pallas kernels for 0% -> 0%
where the time goes in v1:
time: 44.2 us; the launch traced here: 43.9 us
  Pallas kernels  39.3 us (89%)
  local copies, waits for them, and re-layouts  3.34 us (8%)
  between operations  1.29 us (3%)
    pallas_call x1, Pallas kernels, body(): pl.pallas_call(run, out_shape=(jax.ShapeDtypeStruct(incr.shape, F32), jax...  39.3 us
    unnamed x2, local copies, waits for them, and re-layouts  3.34 us

profile of v1, /device:TPU:0, one launch (start us, length us, event | category | flops | bytes accessed | tf_op | source)
XLA Modules:
  0.0 43.9 jit_solution(8964901384708833368)
XLA Ops:
  1.3 39.3 %shard_map.122 = (f32[1,8,192,128]{3,2,1,0:T(8,128)}, f32[8,128]{1,0:T(8,128)}) custom-call(s32[1]{0:T(128)S(6)} %copy.16.refs_0_, f32[1,8,192,128]{3,2,1,0:T(8,128)} %refs_1_.1, bf16[8,1,8,192,128]{4,3,2,1,0:T(8,128)(2,1)} %refs_2_.1, f32[8,128]{1,0:T(8,128)} %bitcast.5, s32[8,192]{1,0:T(8,128)} %refs_4_.1, bf16[1,8,192,128]{3,2,1,0:T(8,128)(2,1)} %refs_5_.1, ...), custom_call_target="tpu_custom_call" | custom-call | tf_op jit(solution)/shard_map/pallas_call | solution.py:387
  40.6 2.1 %copy.17 = f32[1,8,192,128]{3,2,1,0:T(8,128)} copy(f32[1,8,192,128]{3,2,1,0:T(8,128)} %get-tuple-element.10) | data formatting | bytes 1572864
  42.7 1.3 %copy.18 = f32[8,1,128]{2,1,0:T(1,128)} copy(f32[8,1,128]{2,1,0:T(1,128)} %bitcast.4) | data formatting | bytes 8192

commit v2 on v1

--- a/solution.py
+++ b/solution.py
@@ -7,6 +7,7 @@
 
 MESH = pl.DeviceIdType.MESH
 F32, BF16 = jnp.float32, jnp.bfloat16
+GROUP = 2
 LAST = (((1,), (1,)), ((), ()))
 
 
@@ -186,40 +187,40 @@
     loads["m_in"].wait()
     loads["m_out"].wait()
 
-    def forward_row(n, src, dst, r):
-        here = src[r]
-        lap = src[r - 1] + src[r + 1] + pltpu.roll(here, 1, 0) + pltpu.roll(here, LON - 1, 0) - 4.0 * here
-        smoothed = here + diff[r].astype(F32) * lap
-        modes = jnp.dot(smoothed.astype(BF16), m_in[n], preferred_element_type=F32).astype(BF16)
-        advanced = smoothed + jnp.dot(modes, m_out[n], preferred_element_type=F32)
+    def laplacian(field, r, count):
+        here = field[pl.ds(r, count)]
+        sides = pltpu.roll(here, 1, 1) + pltpu.roll(here, LON - 1, 1)
+        return here, field[pl.ds(r - 1, count)] + field[pl.ds(r + 1, count)] + sides - 4.0 * here
+
+    def forward_rows(n, src, dst, r, count):
+        here, lap = laplacian(src, r, count)
+        smoothed = here + diff[pl.ds(r, count)].astype(F32) * lap
+        flat = smoothed.astype(BF16).reshape(count * LON, LEV)
+        modes = jnp.dot(flat, m_in[n], preferred_element_type=F32).astype(BF16)
+        moved = jnp.dot(modes, m_out[n], preferred_element_type=F32)
+        advanced = smoothed + moved.reshape(count, LON, LEV)
         result = jnp.where(n < step_count, advanced, here)
-        dst[r] = result
+        dst[pl.ds(r, count)] = result
         return result
 
     def buffers(n):
         return (a_buf, b_buf) if n % 2 == 0 else (b_buf, a_buf)
 
+    def blocks(row, first, count):
+        done = 0
+        while done < count:
+            size = min(GROUP, count - done)
+            row(first + done, size)
+            done += size
+
     def forward_inner(n):
         src, dst = buffers(n)
-        first, count = H + n + 1, R - 2 * n - 2
-
-        def pair(i, carry):
-            forward_row(n, src, dst, first + i)
-            forward_row(n, src, dst, first + count // 2 + i)
-            return carry
-
-        if count > 0:
-            lax.fori_loop(0, count // 2, pair, 0)
+        blocks(lambda r, c: forward_rows(n, src, dst, r, c), H + n + 1, R - 2 * n - 2)
 
     def forward_edges(n):
         src, dst = buffers(n)
-
-        def pair(i, carry):
-            forward_row(n, src, dst, n + 1 + i)
-            forward_row(n, src, dst, H + R - n - 1 + i)
-            return carry
-
-        lax.fori_loop(0, H, pair, 0)
+        blocks(lambda r, c: forward_rows(n, src, dst, r, c), n + 1, H)
+        blocks(lambda r, c: forward_rows(n, src, dst, r, c), H + R - n - 1, H)
 
     for n in range(H - 1):
         forward_inner(n)
@@ -242,53 +243,40 @@
     got(start_back, has_next)
     src, dst = buffers(H - 1)
 
-    def finish_row(i):
-        end = forward_row(H - 1, src, dst, i + H)
-        misfit = obs[i].astype(F32) * (end - innov[i].astype(F32))
-        seed = misfit - prec_next[i].astype(F32) * (start_next[i].astype(F32) - end)
-        end_bf[i] = end.astype(BF16)
-        u_buf[i + H] = seed
-        seed_bf[i] = seed.astype(BF16)
-
-    def finish(i, carry):
-        finish_row(2 * i)
-        finish_row(2 * i + 1)
-        return carry
-
-    lax.fori_loop(0, H // 2, finish, 0)
+    def finish(i, count):
+        rows = pl.ds(i, count)
+        end = forward_rows(H - 1, src, dst, i + H, count)
+        misfit = obs[rows].astype(F32) * (end - innov[rows].astype(F32))
+        seed = misfit - prec_next[rows].astype(F32) * (start_next[rows].astype(F32) - end)
+        end_bf[rows] = end.astype(BF16)
+        u_buf[pl.ds(i + H, count)] = seed
+        seed_bf[rows] = seed.astype(BF16)
+
+    blocks(finish, 0, H)
     go(seed_up, has_up)
-    lax.fori_loop(H // 2, R // 2, finish, 0)
+    blocks(finish, H, R - H)
     go(seed_down, has_down)
     go(end_on, has_next)
 
-    def couple_row(m, r):
+    def couple(m, r, count):
         n = H - 1 - m
-        here = u_buf[r]
-        modes = lax.dot_general(here.astype(BF16), m_out[n], LAST, preferred_element_type=F32).astype(BF16)
-        coupled = here + lax.dot_general(modes, m_in[n], LAST, preferred_element_type=F32)
-        c_buf[m % 2, r] = coupled
-        w_buf[m % 2, r] = diff[r].astype(F32) * coupled
-
-    def spread_row(m, r):
-        w = w_buf.at[m % 2]
-        here = w[r]
-        lap = w[r - 1] + w[r + 1] + pltpu.roll(here, 1, 0) + pltpu.roll(here, LON - 1, 0) - 4.0 * here
-        u_buf[r] = jnp.where(H - 1 - m < step_count, c_buf[m % 2, r] + lap, u_buf[r])
-
-    def two(row, m, first, second, count):
-        def pair(i, carry):
-            row(m, first + i)
-            row(m, second + i)
-            return carry
-
-        if count > 0:
-            lax.fori_loop(0, count, pair, 0)
+        rows = pl.ds(r, count)
+        here = u_buf[rows]
+        flat = here.astype(BF16).reshape(count * LON, LEV)
+        modes = lax.dot_general(flat, m_out[n], LAST, preferred_element_type=F32).astype(BF16)
+        moved = lax.dot_general(modes, m_in[n], LAST, preferred_element_type=F32)
+        coupled = here + moved.reshape(count, LON, LEV)
+        c_buf[m % 2, rows] = coupled
+        w_buf[m % 2, rows] = diff[rows].astype(F32) * coupled
+
+    def settle(m, r, count):
+        rows = pl.ds(r, count)
+        _, lap = laplacian(w_buf.at[m % 2], r, count)
+        u_buf[rows] = jnp.where(H - 1 - m < step_count, c_buf[m % 2, rows] + lap, u_buf[rows])
 
     for m in range(H):
-        inside = (R - 2 * m) // 2
-        two(couple_row, m, H + m, H + m + inside, inside)
-        inside = (R - 2 * m - 2) // 2
-        two(spread_row, m, H + m + 1, H + m + 1 + inside, inside)
+        blocks(lambda r, c: couple(m, r, c), H + m, R - 2 * m)
+        blocks(lambda r, c: settle(m, r, c), H + m + 1, R - 2 * m - 2)
     got(seed_up, has_down)
     got(seed_down, has_up)
 
@@ -299,8 +287,10 @@
 
     lax.fori_loop(0, H, widen_seed, 0)
     for m in range(H):
-        two(couple_row, m, m, H + R - m, H)
-        two(spread_row, m, m + 1, H + R - m - 1, H)
+        blocks(lambda r, c: couple(m, r, c), m, H)
+        blocks(lambda r, c: couple(m, r, c), H + R - m, H)
+        blocks(lambda r, c: settle(m, r, c), m + 1, H)
+        blocks(lambda r, c: settle(m, r, c), H + R - m - 1, H)
 
     got(end_on, has_prev)
     loads["prec"].wait()
@@ -341,6 +331,28 @@
     sent(start_back, has_prev)
     sent(end_on, has_next)
     store.wait()
+
+
+def deliver(grad_h, owned_h, out_h, gw_ref, buf, small, sem_in, sem_out, sem_small):
+    R = buf.shape[0]
+    pieces = 4 if R % 4 == 0 else 1
+    size = R // pieces
+    ins, outs = [], []
+    for i in range(pieces):
+        rows = pl.ds(i * size, size)
+        ins.append(pltpu.make_async_copy(grad_h.at[0, rows], buf.at[rows], sem_in.at[i]))
+        outs.append(pltpu.make_async_copy(buf.at[rows], out_h.at[0, rows], sem_out.at[i]))
+    fetch = pltpu.make_async_copy(owned_h, small, sem_small.at[0])
+    for copy in ins:
+        copy.start()
+    fetch.start()
+    for arrive, leave in zip(ins, outs):
+        arrive.wait()
+        leave.start()
+    fetch.wait()
+    gw_ref[:, 0, :] = small[...]
+    for copy in outs:
+        copy.wait()
 
 
 def solution(mesh):
@@ -397,7 +409,22 @@
                 collective_id=0, has_side_effects=True, vmem_limit_bytes=60 * 1024 * 1024
             ),
         )(steps, incr, pert, weight[:, 0], cmap, diffusion, m_in, m_out, prec, obs, innov)
-        return grad, owned[:, None]
+        return pl.pallas_call(
+            deliver,
+            out_shape=(
+                jax.ShapeDtypeStruct(incr.shape, F32),
+                jax.ShapeDtypeStruct((MEM, 1, CW), F32),
+            ),
+            in_specs=[pl.BlockSpec(memory_space=pl.ANY)] * 2,
+            out_specs=(pl.BlockSpec(memory_space=pl.ANY), pl.BlockSpec(memory_space=pltpu.VMEM)),
+            scratch_shapes=[
+                field(R, F32),
+                pltpu.VMEM((MEM, CW), F32),
+                pltpu.SemaphoreType.DMA((4,)),
+                pltpu.SemaphoreType.DMA((4,)),
+                pltpu.SemaphoreType.DMA((1,)),
+            ],
+        )(grad, owned)
 
     return jax.shard_map(
         body,

time: 44.2 us -> 36.5 us (0.83)
  Pallas kernels: 39.3 us -> 35 us
  local copies, waits for them, and re-layouts: 3.34 us -> 0 us
    pallas_call x1, Pallas kernels: 39.3 us -> 32.4 us  [body(): pl.pallas_call(run, out_shape=(jax.ShapeDtypeStruct(incr.shape, F32), jax...]
    unnamed x2 -> x0, local copies, waits for them, and re-layouts: 3.34 us -> none
    pallas_call x0 -> x1, Pallas kernels: none -> 2.57 us  [body(): pl.pallas_call(deliver, out_shape=(jax.ShapeDtypeStruct(incr.shape, F32),...]
where the time goes in v2:
time: 36.5 us; the launch traced here: 36.3 us
  Pallas kernels  35 us (96%)
  between operations  1.29 us (4%)
    pallas_call x1, Pallas kernels, body(): pl.pallas_call(run, out_shape=(jax.ShapeDtypeStruct(incr.shape, F32), jax...  32.4 us
    pallas_call x1, Pallas kernels, body(): pl.pallas_call(deliver, out_shape=(jax.ShapeDtypeStruct(incr.shape, F32),...  2.57 us

profile of v2, /device:TPU:0, one launch (start us, length us, event | category | flops | bytes accessed | tf_op | source)
XLA Modules:
  0.0 36.3 jit_solution(8155290152625378518)
XLA Ops:
  1.3 32.4 %shard_map.122 = (f32[1,8,192,128]{3,2,1,0:T(8,128)}, f32[8,128]{1,0:T(8,128)}) custom-call(s32[1]{0:T(128)S(6)} %copy.13.refs_0_, f32[1,8,192,128]{3,2,1,0:T(8,128)} %refs_1_.1, bf16[8,1,8,192,128]{4,3,2,1,0:T(8,128)(2,1)} %refs_2_.1, f32[8,128]{1,0:T(8,128)} %bitcast.1, s32[8,192]{1,0:T(8,128)} %refs_4_.1, bf16[1,8,192,128]{3,2,1,0:T(8,128)(2,1)} %refs_5_.1, ...), custom_call_target="tpu_custom_call" | custom-call | tf_op jit(solution)/shard_map/pallas_call | solution.py:399
  33.7 2.6 %shard_map.123 = (f32[1,8,192,128]{3,2,1,0:T(8,128)}, f32[8,1,128]{2,1,0:T(1,128)}) custom-call(f32[1,8,192,128]{3,2,1,0:T(8,128)} %get-tuple-element.4.grad_h, f32[8,128]{1,0:T(8,128)} %get-tuple-element.5.owned_h), custom_call_target="tpu_custom_call" | custom-call | tf_op jit(solution)/shard_map/pallas_call | solution.py:412

commit v3 on v2

--- a/solution.py
+++ b/solution.py
@@ -114,11 +114,23 @@
     diff_down = remote(1, diff_h.at[0, pl.ds(R - H, H)], diff.at[pl.ds(0, H)], me_t, me_l + 1)
     prec_back = remote(2, prec_h.at[0], prec_next, me_t - 1, me_l)
     start_back = remote(3, start_bf, start_next, me_t - 1, me_l)
-    state_up = remote(4, start_bf.at[pl.ds(0, H)], state_halo.at[1], me_t, me_l - 1)
-    state_down = remote(5, start_bf.at[pl.ds(R - H, H)], state_halo.at[0], me_t, me_l + 1)
-    end_on = remote(6, end_bf, end_prev, me_t + 1, me_l)
-    seed_up = remote(7, seed_bf.at[pl.ds(0, H)], seed_halo.at[1], me_t, me_l - 1)
-    seed_down = remote(8, seed_bf.at[pl.ds(R - H, H)], seed_halo.at[0], me_t, me_l + 1)
+    end_on = remote(4, end_bf, end_prev, me_t + 1, me_l)
+    Q = GROUP if H % GROUP == 0 else 1
+    parts = H // Q
+
+    def edge_copies(base, field, halo):
+        ups, downs = [], []
+        for c in range(parts):
+            first = c * Q
+            ups.append(remote(base + c, field.at[pl.ds(first, Q)], halo.at[1, pl.ds(first, Q)], me_t, me_l - 1))
+            first = H - (c + 1) * Q
+            downs.append(remote(
+                base + parts + c, field.at[pl.ds(R - H + first, Q)], halo.at[0, pl.ds(first, Q)], me_t, me_l + 1
+            ))
+        return ups, downs
+
+    state_up, state_down = edge_copies(5, start_bf, state_halo)
+    seed_up, seed_down = edge_copies(5 + 2 * parts, seed_bf, seed_halo)
 
     def go(copy, there):
         @pl.when(there)
@@ -165,21 +177,32 @@
     loads["pert"].wait()
     loads["incr"].wait()
 
-    def begin(i, carry):
-        cols = mw_t[pl.ds(pl.multiple_of(i * LANES, LANES), LON), :]
-        row = incr[i]
-        for k in range(MEM):
-            row = row + pert[k, i].astype(F32) * cols[:, k:k + 1]
-        start[i] = row
-        a_buf[i + H] = row
-        start_bf[i] = row.astype(BF16)
-        return carry
-
-    lax.fori_loop(0, H, begin, 0)
-    go(state_up, has_up)
-    lax.fori_loop(H, R - H, begin, 0)
-    lax.fori_loop(R - H, R, begin, 0)
-    go(state_down, has_down)
+    def begin(first, count):
+        for i in range(first, first + count):
+            cols = mw_t[i * LANES:i * LANES + LON, :]
+            row = incr[i]
+            for k in range(MEM):
+                row = row + pert[k, i].astype(F32) * cols[:, k:k + 1]
+            start[i] = row
+            a_buf[i + H] = row
+            start_bf[i] = row.astype(BF16)
+
+    def blocks(row, first, count):
+        done = 0
+        while done < count:
+            size = min(GROUP, count - done)
+            row(first + done, size)
+            done += size
+
+    def from_edges(row, ups, downs):
+        for c in range(parts):
+            row(c * Q, Q)
+            go(ups[c], has_up)
+            row(R - (c + 1) * Q, Q)
+            go(downs[c], has_down)
+        blocks(row, H, R - 2 * H)
+
+    from_edges(begin, state_up, state_down)
     go(start_back, has_prev)
 
     step_count = steps_ref[0]
@@ -206,13 +229,6 @@
     def buffers(n):
         return (a_buf, b_buf) if n % 2 == 0 else (b_buf, a_buf)
 
-    def blocks(row, first, count):
-        done = 0
-        while done < count:
-            size = min(GROUP, count - done)
-            row(first + done, size)
-            done += size
-
     def forward_inner(n):
         src, dst = buffers(n)
         blocks(lambda r, c: forward_rows(n, src, dst, r, c), H + n + 1, R - 2 * n - 2)
@@ -226,8 +242,10 @@
         forward_inner(n)
     got(diff_up, has_down)
     got(diff_down, has_up)
-    got(state_up, has_down)
-    got(state_down, has_up)
+    for copy in state_up:
+        got(copy, has_down)
+    for copy in state_down:
+        got(copy, has_up)
 
     def widen(i, carry):
         a_buf[i] = state_halo[0, i].astype(F32)
@@ -252,10 +270,7 @@
         u_buf[pl.ds(i + H, count)] = seed
         seed_bf[rows] = seed.astype(BF16)
 
-    blocks(finish, 0, H)
-    go(seed_up, has_up)
-    blocks(finish, H, R - H)
-    go(seed_down, has_down)
+    from_edges(finish, seed_up, seed_down)
     go(end_on, has_next)
 
     def couple(m, r, count):
@@ -277,8 +292,10 @@
     for m in range(H):
         blocks(lambda r, c: couple(m, r, c), H + m, R - 2 * m)
         blocks(lambda r, c: settle(m, r, c), H + m + 1, R - 2 * m - 2)
-    got(seed_up, has_down)
-    got(seed_down, has_up)
+    for copy in seed_up:
+        got(copy, has_down)
+    for copy in seed_down:
+        got(copy, has_up)
 
     def widen_seed(i, carry):
         u_buf[i] = seed_halo[0, i].astype(F32)
@@ -307,13 +324,18 @@
 
     store = local(10, grad, grad_h.at[0])
     store.start()
-    sums = lax.dot_general(halves(contrib[...]), onehot[...], LAST, preferred_element_type=F32)
-    sums = sums[0:MEM] + sums[MEM:2 * MEM]
-    for p in range(tm_count):
-        term_send[p] = sums[:, p * CW:(p + 1) * CW]
-    for d in range(1, tm_count):
+    pieces = halves(contrib[...])
+
+    def owed(p):
+        block = onehot[pl.ds(pl.multiple_of(p * CW, CW), CW), :]
+        both = lax.dot_general(pieces, block, LAST, preferred_element_type=F32)
+        return both[0:MEM] + both[MEM:2 * MEM]
+
+    for d in sorted(range(1, tm_count), key=lambda d: -min(d, tm_count - d)):
+        peer = lax.rem(me_t + d, tm_count)
+        term_send[peer] = owed(peer)
         term(d).start()
-    result = gathered[me_t] + term_send[me_t]
+    result = gathered[me_t] + owed(me_t)
     for d in range(1, tm_count):
         term(d).wait_recv()
     for d in range(1, tm_count):
@@ -323,9 +345,9 @@
     for d in range(1, tm_count):
         spread(d).wait_send()
         term(d).wait_send()
-    for copy in (diff_up, state_up, seed_up):
+    for copy in [diff_up] + state_up + seed_up:
         sent(copy, has_up)
-    for copy in (diff_down, state_down, seed_down):
+    for copy in [diff_down] + state_down + seed_down:
         sent(copy, has_down)
     sent(prec_back, has_prev)
     sent(start_back, has_prev)
@@ -389,8 +411,8 @@
             pltpu.VMEM((tm_count, MEM, CW), F32),
             pltpu.VMEM((tm_count, MEM, CW), F32),
             pltpu.SemaphoreType.DMA((11,)),
-            pltpu.SemaphoreType.DMA((9,)),
-            pltpu.SemaphoreType.DMA((9,)),
+            pltpu.SemaphoreType.DMA((5 + 4 * H,)),
+            pltpu.SemaphoreType.DMA((5 + 4 * H,)),
         ] + [pltpu.SemaphoreType.DMA((tm_count,))] * 4
 
         def run(*refs):

time: 36.5 us -> 37 us (1.014)
  Pallas kernels: 35 us -> 35.4 us
where the time goes in v3:
time: 37 us; the launch traced here: 36.7 us
  Pallas kernels  35.4 us (96%)
  between operations  1.29 us (3%)
    pallas_call x1, Pallas kernels, body(): pl.pallas_call(run, out_shape=(jax.ShapeDtypeStruct(incr.shape, F32), jax...  32.8 us
    pallas_call x1, Pallas kernels, body(): pl.pallas_call(deliver, out_shape=(jax.ShapeDtypeStruct(incr.shape, F32),...  2.57 us

profile of v3, /device:TPU:0, one launch (start us, length us, event | category | flops | bytes accessed | tf_op | source)
XLA Modules:
  0.0 36.7 jit_solution(487814247749873449)
XLA Ops:
  1.3 32.8 %shard_map.122 = (f32[1,8,192,128]{3,2,1,0:T(8,128)}, f32[8,128]{1,0:T(8,128)}) custom-call(s32[1]{0:T(128)S(6)} %copy.13.refs_0_, f32[1,8,192,128]{3,2,1,0:T(8,128)} %refs_1_.1, bf16[8,1,8,192,128]{4,3,2,1,0:T(8,128)(2,1)} %refs_2_.1, f32[8,128]{1,0:T(8,128)} %bitcast.1, s32[8,192]{1,0:T(8,128)} %refs_4_.1, bf16[1,8,192,128]{3,2,1,0:T(8,128)(2,1)} %refs_5_.1, ...), custom_call_target="tpu_custom_call" | custom-call | tf_op jit(solution)/shard_map/pallas_call | solution.py:421
  34.1 2.6 %shard_map.123 = (f32[1,8,192,128]{3,2,1,0:T(8,128)}, f32[8,1,128]{2,1,0:T(1,128)}) custom-call(f32[1,8,192,128]{3,2,1,0:T(8,128)} %get-tuple-element.4.grad_h, f32[8,128]{1,0:T(8,128)} %get-tuple-element.5.owned_h), custom_call_target="tpu_custom_call" | custom-call | tf_op jit(solution)/shard_map/pallas_call | solution.py:434
